TPU v7x, 32 devices: a whole 2x2x4 slice. The times are simulated.
32 devices in a mesh: wide: 8 (over z, x), narrow: 4 (over y, core).
Axes of the slice: x: 2, y: 2, z: 4, core: 2. Of those that a mesh axis runs over, the one named last changes fastest.
Arguments:
- table: float32 [256, 256, 64, 128], P(None, 'narrow', 'wide'), may hold values from -200 to 200, as said below
- prior_one: float32 [256, 32], replicated, may hold values from -0.375 to 0.375
- factor_two: float32 [256, 32], replicated, may hold values from -0.375 to 0.375
- factor_three: float32 [64, 32], replicated, may hold values from -0.75 to 0.75
Outputs:
- core: float32 [32, 32, 32, 128], P('narrow', 'wide')
- basis: float32 [256, 32], replicated
Inputs may be any that keep to these rules, and one draw needn't show every extreme that they name: Entries of the table lie within the stated bounds.
All inputs are finite; a program needn't handle non-finite values.
Results may differ from a plain program's by a relative error of at most 0.0003.
Values sent between devices are 32-bit elements; how exact they have to be, the bound alone decides.
A program may use at most 256 MiB of HBM per device.

v0:
```python
import jax
import jax.numpy as jnp
from jax import lax
from jax.sharding import PartitionSpec as P

I2 = 256
I3 = 64
M = 128
SUB = 2
HIGH = lax.Precision.HIGHEST


def orthonormal(q):
    s = jnp.dot(q.T, q, precision=HIGH, preferred_element_type=jnp.float32)
    lower = jnp.linalg.cholesky(s)
    return lax.linalg.triangular_solve(lower, q, left_side=False, lower=True, transpose_a=True)


def per_device(table, prior_one, factor_two, factor_three):
    order_one = table.shape[0]
    rows_two, rows_three, cells = (table.shape[1], table.shape[2], table.shape[3])
    flat = table.reshape(order_one, rows_two * rows_three * cells)
    scale = 1.0 / float(I2 * I3 * M)
    basis = prior_one
    partial_value = jnp.dot(flat, flat.T, precision=HIGH, preferred_element_type=jnp.float32)
    gram = lax.psum(partial_value, ("wide", "narrow")) / scale ** (-1)
    for step in range(SUB):
        basis = orthonormal(
            jnp.dot(gram, basis, precision=HIGH, preferred_element_type=jnp.float32)
        )
    rank = basis.shape[1]
    cut_off = jnp.dot(basis.T, flat, precision=HIGH, preferred_element_type=jnp.float32)
    cut_off = cut_off.reshape(rank, rows_two, rows_three, cells)
    regrouped = lax.all_to_all(cut_off, "narrow", split_axis=0, concat_axis=1, tiled=True)
    second = jnp.einsum("aijm,ib->abjm", regrouped, factor_two, precision=HIGH)
    start = lax.axis_index("wide") * rows_three
    local_three = lax.dynamic_slice_in_dim(factor_three, start, rows_three, 0)
    terms = jnp.einsum("abjm,jc->abcm", second, local_three, precision=HIGH)
    core = lax.psum_scatter(terms, "wide", scatter_dimension=1, tiled=True)
    return (core, basis)


def solution(mesh):
    return jax.shard_map(
        per_device,
        mesh=mesh,
        in_specs=(P(None, "narrow", "wide", None), P(), P(), P()),
        out_specs=(P("narrow", "wide", None, None), P()),
        check_vma=False,
    )
```

profile of v0, /device:TPU:0, one launch (start us, length us, event | category | flops | bytes accessed | tf_op | source)
XLA Modules:
  0.0 652.3 jit_solution(17600477769189699123)
XLA Ops:
  7.2 150.5 %fusion.7 = f32[256,256]{1,0:T(8,128)} fusion(f32[256,64,8,128]{3,2,1,0:T(8,128)} %param.7), kind=kOutput, calls=%fused_computation.7 | convolution fusion | flops 51539607552 | bytes 67371008 | tf_op jit(solution)/shard_map/dot_general | solution.py:25
  157.8 56.5 %copy.57 = f32[32,8,512,128]{3,1,2,0:T(8,128)} copy(f32[32,8,512,128]{3,2,1,0:T(8,128)} %bitcast.38) | data formatting | bytes 134217728
  214.2 65.9 %copy.33 = f32[65536,256]{1,0:T(8,128)} copy(f32[65536,256]{0,1:T(8,128)} %bitcast.74) | data formatting | bytes 134217728 | tf_op jit(solution)/shard_map/dot_general | solution.py:32
  280.2 5.5 all-reduce.4.cloned.1.call-done
  285.6 1.3 fusion.13
  287.2 2.9 cholesky.44
  290.1 0.6 compare_reduce_fusion.1
  290.8 0.7 fusion.20
  291.4 2.4 custom-call.6
  294.1 1.3 fusion.11
  295.7 2.9 cholesky.55
  298.6 0.6 compare_reduce_fusion
  299.3 0.7 fusion.21
  299.9 2.4 custom-call.7
  302.6 63.7 %fusion.18 = f32[32,64,8,128]{3,0,2,1:T(8,128)S(1)} fusion(f32[64,8,128,256]{3,2,1,0:T(8,128)} %bitcast.15, f32[32,256]{1,0:T(8,128)S(1)} %fusion.23), kind=kOutput, calls=%fused_computation.17 | convolution fusion | flops 6442450944 | bytes 75530240 | tf_op jit(solution)/shard_map/dot_general | solution.py:32
  366.4 8.1 %copy.34 = f32[32,64,8,128]{3,2,1,0:T(8,128)} copy(f32[32,64,8,128]{3,0,2,1:T(8,128)S(1)} %fusion.18) | data formatting | bytes 16777216 | tf_op jit(solution)/shard_map/dot_general | solution.py:32
  374.4 5.7 all-to-all-start
  380.1 93.1 %all-to-all-done = f32[32,64,8,128]{3,2,1,0:T(8,128)} async-done(((f32[32,64,8,128]{3,2,1,0:T(8,128)}), f32[32,64,8,128]{3,2,1,0:T(8,128)}, u32[]{:S(2)}, u32[]{:S(2)}) %all-to-all-start) | async-done | bytes 8388640 | tf_op jit(solution)/shard_map/all_to_all | solution.py:34
  473.3 3.9 copy.35
  477.3 5.8 fusion.4
  483.1 5.1 convolution_bitcast_fusion
  488.1 0.6 dynamic-slice
  489.4 154.2 %all-reduce.6.cloned.1.call-done = f32[8,32,32,128]{3,2,1,0:T(8,128)} async-done(((f32[8,32,32,128]{3,2,1,0:T(8,128)}), f32[8,32,32,128]{3,2,1,0:T(8,128)}) %all-reduce.6.cloned.1.call-update) | async-done | bytes 4194320
  643.6 1.9 constant_dynamic-slice_fusion
  (24 shorter events, 1.2 us)
Async XLA Ops:
  7.2 470.1 %copy-start = (f32[256,32]{0,1:T(8,128)S(1)}, f32[256,32]{0,1:T(8,128)}, u32[]{:S(2)}) copy-start(f32[256,32]{0,1:T(8,128)} %param.9) | copy-start | bytes 98308
  7.2 278.4 %all-reduce.4.cloned.1.call-start = ((), (), s32[]{:S(2)}) async-start(), calls=%async_computation.1 | async-start | bytes 524288 | tf_op jit(solution)/shard_map/psum | solution.py:26
  214.2 71.4 %copy-start.2 = (f32[256,32]{0,1:T(8,128)S(1)}, f32[256,32]{0,1:T(8,128)}, u32[]{:S(2)}) copy-start(f32[256,32]{0,1:T(8,128)} %param.8) | copy-start | bytes 98308
  302.6 63.7 %copy-start.1 = (f32[32,256]{1,0:T(8,128)}, f32[32,256]{1,0:T(8,128)S(1)}, u32[]{:S(2)}) copy-start(f32[32,256]{1,0:T(8,128)S(1)} %fusion.23) | copy-start | bytes 98308
  374.4 98.8 %all-to-all-start = ((f32[32,64,8,128]{3,2,1,0:T(8,128)}), f32[32,64,8,128]{3,2,1,0:T(8,128)}, u32[]{:S(2)}, u32[]{:S(2)}) async-start(f32[32,64,8,128]{3,2,1,0:T(8,128)} %copy.34), calls=%async_computation | async-start | bytes 16777216 | tf_op jit(solution)/shard_map/all_to_all | solution.py:34
  380.1 263.5 %all-reduce.6.cloned.1.call-start = ((), (), s32[]{:S(2)}) async-start(), calls=%async_computation.2 | async-start | bytes 8388608
  477.2 5.8 copy-start.3
  477.2 10.9 %copy-start.4 = (u32[32]{0:T(128)S(1)}, u32[32]{0:T(128)}, u32[]{:S(2)}) copy-start(u32[32]{0:T(128)} %constant.46) | copy-start | bytes 388
Sparse Core Ops, SparseCore 0:
  157.9 127.6 all-reduce.3
  488.3 155.2 all-reduce.5
where the time goes:
time: 653 us; the launch traced here: 652 us
  waiting for transfers between devices  253 us (39%)
  matrix products  228 us (35%)
  local copies, waits for them, and re-layouts  137 us (21%)
  between operations  14.9 us (2%)
  other arithmetic  13.4 us (2%)
    unnamed x3, waiting for transfers between devices  154 us
    dot_general x1, matrix products, per_device(): jnp.dot(flat, flat.T, precision=HIGH, preferred_element_type=jnp.float32)  151 us
    all_to_all x1, waiting for transfers between devices, per_device(): lax.all_to_all(cut_off, 'narrow', split_axis=0, concat_axis=1, tiled=True)  93.1 us
    dot_general x2, local copies, waits for them, and re-layouts, per_device(): jnp.dot(basis.T, flat, precision=HIGH, preferred_element_type=jnp.float32)  74 us
    dot_general x1, matrix products, per_device(): jnp.dot(basis.T, flat, precision=HIGH, preferred_element_type=jnp.float32)  63.7 us
    unnamed x13, local copies, waits for them, and re-layouts  58.9 us
  transfers between devices with their start and end apart: 3, of which 3 were waited for; matrix products, arithmetic and copies ran while one was open for 19% of the time, Pallas kernels for 0%

commit v1 on v0

--- a/solution.py
+++ b/solution.py
@@ -31,7 +31,12 @@
     rank = basis.shape[1]
     cut_off = jnp.dot(basis.T, flat, precision=HIGH, preferred_element_type=jnp.float32)
     cut_off = cut_off.reshape(rank, rows_two, rows_three, cells)
-    regrouped = lax.all_to_all(cut_off, "narrow", split_axis=0, concat_axis=1, tiled=True)
+    regrouped = jnp.concatenate(
+        lax.all_to_all(
+            jnp.stack(jnp.split(cut_off, lax.axis_size("narrow"), axis=0)), "narrow", 0, 0
+        ),
+        axis=1,
+    )
     second = jnp.einsum("aijm,ib->abjm", regrouped, factor_two, precision=HIGH)
     start = lax.axis_index("wide") * rows_three
     local_three = lax.dynamic_slice_in_dim(factor_three, start, rows_three, 0)

time: 653 us -> 706 us (1.081); the launches traced: 652 us -> 698 us
  local copies, waits for them, and re-layouts: 137 us -> 6.63 us
  waiting for transfers between devices: 253 us -> 375 us
  matrix products: 228 us -> 278 us
    psum x1, waiting for transfers between devices: 5.47 us -> 128 us  [per_device(): gram = lax.psum(partial_value, ('wide', 'narrow')) / scale ** (-1)]
    dot_general x2 -> x0, local copies, waits for them, and re-layouts: 74 us -> none  [per_device(): jnp.dot(basis.T, flat, precision=HIGH, preferred_element_type=jnp.float32)]
    unnamed x13 -> x12, local copies, waits for them, and re-layouts: 58.9 us -> 2.48 us
    dot_general x1, matrix products: 63.7 us -> 106 us  [per_device(): jnp.dot(basis.T, flat, precision=HIGH, preferred_element_type=jnp.float32)]
  transfers between devices with their start and end apart: 3 -> 3, of which waited for: 3 -> 3; matrix products, arithmetic and copies ran while one was open for 19% -> 0% of each run, Pallas kernels for 0% -> 0%
where the time goes in v1:
time: 706 us; the launch traced here: 698 us
  waiting for transfers between devices  375 us (53%)
  matrix products  278 us (39%)
  other arithmetic  16.9 us (2%)
  between operations  15.2 us (2%)
    unnamed x3, waiting for transfers between devices  154 us
    dot_general x1, matrix products, per_device(): jnp.dot(flat, flat.T, precision=HIGH, preferred_element_type=jnp.float32)  151 us
    psum x1, waiting for transfers between devices, per_device(): gram = lax.psum(partial_value, ('wide', 'narrow')) / scale ** (-1)  128 us
    dot_general x1, matrix products, per_device(): jnp.dot(basis.T, flat, precision=HIGH, preferred_element_type=jnp.float32)  106 us
    all_to_all x1, waiting for transfers between devices, per_device(): lax.all_to_all(jnp.stack(jnp.split(cut_off, lax.axis_size('narrow'), axis...  93.1 us
  transfers between devices with their start and end apart: 3, of which 3 were waited for; matrix products, arithmetic and copies ran while one was open for 0% of the time, Pallas kernels for 0%

profile of v1, /device:TPU:0, one launch (start us, length us, event | category | flops | bytes accessed | tf_op | source)
XLA Modules:
  0.0 697.8 jit_solution(14789900582828672784)
XLA Ops:
  7.2 150.5 %fusion.7 = f32[256,256]{1,0:T(8,128)} fusion(f32[256,64,8,128]{3,2,1,0:T(8,128)} %param.7), kind=kOutput, calls=%fused_computation.9 | convolution fusion | flops 51539607552 | bytes 67371008 | tf_op jit(solution)/shard_map/dot_general | solution.py:25
  157.8 127.9 %all-reduce.4.cloned.1.call-done = f32[256,256]{1,0:T(8,128)} async-done(((f32[256,256]{1,0:T(8,128)}), f32[256,256]{1,0:T(8,128)}) %all-reduce.4.cloned.1.call-update) | async-done | bytes 262160 | tf_op jit(solution)/shard_map/psum | solution.py:26
  285.7 1.3 fusion.14
  287.2 2.9 cholesky.44
  290.2 0.6 compare_reduce_fusion.1
  290.8 0.7 fusion.19
  291.5 2.4 custom-call.6
  293.9 0.2 convolution_bitcast_fusion.2
  294.2 1.3 fusion.12
  295.7 2.9 cholesky.55
  298.7 0.6 compare_reduce_fusion
  299.3 0.7 fusion.20
  300.0 2.4 custom-call.7
  302.4 0.2 convolution_bitcast_fusion.1
  302.7 106.5 %fusion = f32[32,65536]{1,0:T(8,128)} fusion(f32[256,32]{0,1:T(8,128)S(1)} %convolution_bitcast_fusion.1, f32[32,8,512,128]{3,2,1,0:T(8,128)} %bitcast.35), kind=kOutput, calls=%fused_computation | convolution fusion | flops 6442450944 | bytes 75530240 | tf_op jit(solution)/shard_map/dot_general | solution.py:32
  409.2 4.0 fusion.32
  413.2 3.5 pad_maximum_fusion
  416.7 5.7 all-to-all-start
  422.4 93.1 %all-to-all-done = f32[4,8,64,8,128]{4,1,3,2,0:T(8,128)} async-done(((f32[4,8,64,8,128]{4,1,3,2,0:T(8,128)}), f32[4,8,64,8,128]{4,1,3,2,0:T(8,128)}, u32[]{:S(2)}, u32[]{:S(2)}) %all-to-all-start) | async-done | bytes 8388640 | tf_op jit(solution)/shard_map/all_to_all | solution.py:35
  515.6 12.6 %fusion.5 = f32[8,8,128,32]{2,3,1,0:T(8,128)S(1)} fusion(f32[8,256,8,128]{3,0,2,1:T(8,128)} %bitcast.17, f32[256,32]{0,1:T(8,128)S(1)} %copy-done), kind=kOutput, calls=%fused_computation.6 | convolution fusion | flops 805306368 | bytes 9469952 | tf_op jit(solution)/shard_map/aijm,ib->abjm/dot_general | solution.py:40
  528.2 5.1 convolution_bitcast_fusion
  533.3 0.6 dynamic-slice
  534.6 154.2 %all-reduce.6.cloned.1.call-done = f32[8,32,32,128]{3,2,1,0:T(8,128)} async-done(((f32[8,32,32,128]{3,2,1,0:T(8,128)}), f32[8,32,32,128]{3,2,1,0:T(8,128)}) %all-reduce.6.cloned.1.call-update) | async-done | bytes 4194320
  688.7 1.9 constant_dynamic-slice_fusion
  (22 shorter events, 0.7 us)
Async XLA Ops:
  7.2 508.4 %copy-start = (f32[256,32]{0,1:T(8,128)S(1)}, f32[256,32]{0,1:T(8,128)}, u32[]{:S(2)}) copy-start(f32[256,32]{0,1:T(8,128)} %param.9) | copy-start | bytes 98308
  7.2 278.5 %copy-start.2 = (f32[256,32]{0,1:T(8,128)S(1)}, f32[256,32]{0,1:T(8,128)}, u32[]{:S(2)}) copy-start(f32[256,32]{0,1:T(8,128)} %param.8) | copy-start | bytes 98308
  7.2 278.5 %all-reduce.4.cloned.1.call-start = ((), (), s32[]{:S(2)}) async-start(), calls=%async_computation.1 | async-start | bytes 524288 | tf_op jit(solution)/shard_map/psum | solution.py:26
  302.7 106.5 %copy-start.1 = (f32[256,32]{0,1:T(8,128)}, f32[256,32]{0,1:T(8,128)S(1)}, u32[]{:S(2)}) copy-start(f32[256,32]{0,1:T(8,128)S(1)} %convolution_bitcast_fusion.1) | copy-start | bytes 98308
  416.7 98.8 %all-to-all-start = ((f32[4,8,64,8,128]{4,1,3,2,0:T(8,128)}), f32[4,8,64,8,128]{4,1,3,2,0:T(8,128)}, u32[]{:S(2)}, u32[]{:S(2)}) async-start(f32[4,8,64,8,128]{4,1,3,2,0:T(8,128)} %pad_maximum_fusion), calls=%async_computation | async-start | bytes 16777216 | tf_op jit(solution)/shard_map/all_to_all | solution.py:35
  422.4 105.8 %copy-start.3 = (f32[64,32]{0,1:T(8,128)S(1)}, f32[64,32]{0,1:T(8,128)}, u32[]{:S(2)}) copy-start(f32[64,32]{0,1:T(8,128)} %param.10) | copy-start | bytes 24580
  422.4 266.3 %all-reduce.6.cloned.1.call-start = ((), (), s32[]{:S(2)}) async-start(), calls=%async_computation.2 | async-start | bytes 8388608
  515.6 17.8 %copy-start.4 = (u32[32]{0:T(128)S(1)}, u32[32]{0:T(128)}, u32[]{:S(2)}) copy-start(u32[32]{0:T(128)} %constant.46) | copy-start | bytes 388
Sparse Core Ops, SparseCore 0:
  157.9 127.7 all-reduce.3
  533.4 155.2 all-reduce.5
